TPU v7x, 256 devices: a whole 4x4x8 slice. The times are simulated.
256 devices in a mesh: expert: 16 (over y, x), hidden: 16 (over z, core).
Axes of the slice: x: 4, y: 4, z: 8, core: 2. Of those that a mesh axis runs over, the one named last changes fastest.
Arguments:
- layer_input: bfloat16 [4096, 4096], P('expert', 'hidden'), may hold values from -6 to 6
- output_grad: bfloat16 [4096, 4096], P('expert', 'hidden'), may hold values from -1.5 to 1.5
- latent_saved: bfloat16 [4096, 1024], P('expert'), may hold values from -6 to 6
- combined_saved: bfloat16 [4096, 1024], P('expert'), may hold values from -6 to 6
- expert_ids: int32 [4096, 22], P('expert'), may hold values from 0 to 511, as said below
- gate_values: bfloat16 [4096, 22], P('expert'), may hold values from 0.099609375 to 1.5
- down_proj: bfloat16 [1024, 4096], P(None, 'hidden'), may hold values from -0.09375 to 0.09375
- up_proj: bfloat16 [1024, 4096], P(None, 'hidden'), may hold values from -0.1875 to 0.1875
- expert_in: bfloat16 [16, 1024, 2688], P('expert', None, 'hidden'), may hold values from -0.1875 to 0.1875
- expert_out: bfloat16 [16, 2688, 1024], P('expert', 'hidden'), may hold values from -0.125 to 0.125
Outputs:
- input_grad: bfloat16 [4096, 4096], P('expert', 'hidden')
- down_grad: float32 [1024, 4096], P('expert', 'hidden')
- up_grad: float32 [1024, 4096], P('expert', 'hidden')
- gate_grad: float32 [4096, 22], P('expert')
- expert_in_grad: float32 [16, 1024, 2688], P('expert', None, 'hidden')
- expert_out_grad: float32 [16, 2688, 1024], P('expert', 'hidden')
Inputs may be any that keep to these rules, and one draw needn't show every extreme that they name: `expert_ids`: each row names 22 different experts. In each aligned block of 256 rows (the rows of one index of the expert axis) each expert below 16 is named by at most 24 rows; some expert below 16 is named by exactly 24 rows in every block.
All inputs are finite; a program needn't handle non-finite values.
Results may differ from a plain program's by a relative error of at most 0.0065.
Values may be sent and summed in bfloat16 or wider, within the bound.
No kernel may reach another device: no remote copies, remote signals or barrier semaphores. Data moves between devices by JAX's collectives and lax.ppermute only.
A program may use at most 64 MiB of HBM per device.

v0:
```python
import jax
import jax.numpy as jnp
from jax import lax
from jax.sharding import PartitionSpec as P


def slot_layout(table, groups, local_count):
    tokens_here = table.shape[0]
    return table.T.reshape(groups, local_count, tokens_here).transpose(1, 0, 2)[:, :, None, :]


def on_device(
    layer_input,
    output_grad,
    latent_saved,
    combined_saved,
    expert_ids,
    gate_values,
    down_proj,
    up_proj,
    expert_in,
    expert_out,
):
    groups = lax.axis_size("expert")
    tokens_here = layer_input.shape[0]
    latent_width = latent_saved.shape[1]
    local_count = expert_in.shape[0]
    capacity = tokens_here * 3 // 32
    live_count = local_count * groups
    slot_total = local_count * groups * capacity
    partial_cot = jnp.einsum("td,ld->tl", output_grad, up_proj, preferred_element_type=jnp.float32)
    member = expert_ids[:, :, None] == jnp.arange(live_count, dtype=jnp.int32)[None, None, :]
    per_token = jnp.sum(member.astype(jnp.int32), axis=1)
    before = jnp.cumsum(per_token, axis=0) - per_token
    gate_token = jnp.sum(
        jnp.where(member, gate_values.astype(jnp.float32)[:, :, None], 0.0), axis=1
    )
    rank_iota = jnp.arange(capacity, dtype=jnp.int32)[None, None, :, None]
    hit_slot = (slot_layout(per_token, groups, local_count) == 1) & (
        slot_layout(before, groups, local_count) == rank_iota
    )
    gate_slot = jnp.sum(
        jnp.where(hit_slot, slot_layout(gate_token, groups, local_count), 0.0), axis=3
    )
    gate_send = gate_slot.astype(jnp.bfloat16)
    dispatch_bf = hit_slot.astype(jnp.bfloat16).reshape(slot_total, tokens_here)
    cot_full = lax.psum(partial_cot, "hidden")
    cot_rows = jnp.dot(
        dispatch_bf, cot_full.astype(jnp.bfloat16), preferred_element_type=jnp.float32
    ).astype(jnp.bfloat16)
    latent_rows = jnp.dot(dispatch_bf, latent_saved, preferred_element_type=jnp.float32).astype(
        jnp.bfloat16
    )
    cot_recv, latent_recv, gate_recv = (
        lax.all_to_all(
            cot_rows.reshape(local_count, groups, capacity, latent_width),
            "expert",
            split_axis=1,
            concat_axis=1,
            tiled=True,
        ),
        lax.all_to_all(
            latent_rows.reshape(local_count, groups, capacity, latent_width),
            "expert",
            split_axis=1,
            concat_axis=1,
            tiled=True,
        ),
        lax.all_to_all(gate_send, "expert", split_axis=1, concat_axis=1, tiled=True),
    )
    row_count = groups * capacity
    cot_block = cot_recv.reshape(local_count, row_count, latent_width)
    latent_block = latent_recv.reshape(local_count, row_count, latent_width)
    gate_block = gate_recv.reshape(local_count, row_count).astype(jnp.float32)
    pre_act = jnp.einsum(
        "erl,elf->erf", latent_block, expert_in, preferred_element_type=jnp.float32
    )
    relu_out = jnp.maximum(pre_act, 0.0)
    back_proj = jnp.einsum(
        "erl,efl->erf", cot_block, expert_out, preferred_element_type=jnp.float32
    )
    gate_part = jnp.sum(back_proj * relu_out * relu_out, axis=2)
    scaled_act = (gate_block[:, :, None] * relu_out * relu_out).astype(jnp.bfloat16)
    pre_grad = (2.0 * gate_block[:, :, None] * relu_out * back_proj).astype(jnp.bfloat16)
    expert_out_grad = jnp.einsum(
        "erf,erl->efl", scaled_act, cot_block, preferred_element_type=jnp.float32
    )
    expert_in_grad = jnp.einsum(
        "erl,erf->elf", latent_block, pre_grad, preferred_element_type=jnp.float32
    )
    latent_back = jnp.einsum(
        "erf,elf->erl", pre_grad, expert_in, preferred_element_type=jnp.float32
    )
    latent_back = latent_back.reshape(local_count, groups, capacity, latent_width)
    gate_part = gate_part.reshape(local_count, groups, capacity)
    dispatch_full = hit_slot.astype(jnp.float32)
    dispatch_flat = dispatch_full.reshape(slot_total, tokens_here)
    rows_home, gate_home = (
        lax.all_to_all(latent_back, "expert", split_axis=1, concat_axis=1, tiled=True),
        lax.all_to_all(gate_part, "expert", split_axis=1, concat_axis=1, tiled=True),
    )
    token_sums = jnp.dot(
        dispatch_flat.T,
        rows_home.reshape(slot_total, latent_width),
        precision=lax.Precision.HIGHEST,
        preferred_element_type=jnp.float32,
    )
    by_expert = jnp.sum(dispatch_full * gate_home[:, :, :, None], axis=2)
    by_expert = by_expert.transpose(2, 1, 0).reshape(tokens_here, live_count)
    gate_local = jnp.sum(jnp.where(member, by_expert[:, None, :], 0.0), axis=2)
    latent_grad, gate_grad = lax.psum((token_sums, gate_local), "hidden")
    latent_bf = latent_grad.astype(jnp.bfloat16)
    input_grad = jnp.dot(latent_bf, down_proj, preferred_element_type=jnp.float32).astype(
        jnp.bfloat16
    )
    down_term = jnp.einsum("tl,td->ld", latent_bf, layer_input, preferred_element_type=jnp.float32)
    up_term = jnp.einsum(
        "tl,td->ld", combined_saved, output_grad, preferred_element_type=jnp.float32
    )
    down_grad, up_grad = (
        lax.psum_scatter(down_term, "expert", scatter_dimension=0, tiled=True),
        lax.psum_scatter(up_term, "expert", scatter_dimension=0, tiled=True),
    )
    return (input_grad, down_grad, up_grad, gate_grad, expert_in_grad, expert_out_grad)


def solution(mesh):
    return jax.shard_map(
        on_device,
        mesh=mesh,
        in_specs=(
            P("expert", "hidden"),
            P("expert", "hidden"),
            P("expert", None),
            P("expert", None),
            P("expert", None),
            P("expert", None),
            P(None, "hidden"),
            P(None, "hidden"),
            P("expert", None, "hidden"),
            P("expert", "hidden", None),
        ),
        out_specs=(
            P("expert", "hidden"),
            P("expert", "hidden"),
            P("expert", "hidden"),
            P("expert", None),
            P("expert", None, "hidden"),
            P("expert", "hidden", None),
        ),
        check_vma=False,
    )
```

profile of v0, /device:TPU:2, one launch (start us, length us, event | category | flops | bytes accessed | tf_op | source)
XLA Modules:
  0.0 312.9 jit_solution(7600036610667485425)
XLA Ops:
  7.2 0.0 copy-start
  7.2 0.8 convert_reduce_fusion
  8.1 0.1 eq.79
  8.1 0.6 reduce-window.6
  8.7 0.2 slice_reduce_fusion
  9.0 0.1 bitcast_subtract_fusion
  9.0 1.5 fusion.23
  10.5 62.0 %all-reduce.3 = bf16[256,1024]{1,0:T(8,128)(2,1)S(1)} all-reduce(f32[256,1024]{1,0:T(8,128)S(1)} %fusion.23), channel_id=1, replica_groups=mesh['expert'=16,'hidden'=16] {'hidden'}, use_global_device_ids=true, to_apply=%region_5.6 | all-reduce | flops 262144 | bytes 1572864 | tf_op jit(solution)/shard_map/psum | solution.py:47
  72.5 0.1 fusion.9
  72.7 1.3 convolution_convert_fusion
  73.9 7.5 %all-to-all-start.2 = ((bf16[1,16,24,1024]{3,2,0,1:T(8,128)(2,1)}), bf16[1,16,24,1024]{3,2,0,1:T(8,128)(2,1)S(1)}, u32[]{:S(2)}, u32[]{:S(2)}) async-start(bf16[1,16,24,1024]{3,2,0,1:T(8,128)(2,1)} %bitcast.11), calls=%async_computation.2 | async-start | bytes 1572864 | tf_op jit(solution)/shard_map/all_to_all | solution.py:55
  81.4 0.0 copy-done
  81.4 0.0 copy-start.5
  81.4 1.3 convolution_convert_fusion.1
  82.7 0.0 copy-start.1
  82.7 8.9 %all-to-all-done.2 = bf16[1,16,24,1024]{3,2,0,1:T(8,128)(2,1)S(1)} async-done(((bf16[1,16,24,1024]{3,2,0,1:T(8,128)(2,1)}), bf16[1,16,24,1024]{3,2,0,1:T(8,128)(2,1)S(1)}, u32[]{:S(2)}, u32[]{:S(2)}) %all-to-all-start.2) | async-done | bytes 786464 | tf_op jit(solution)/shard_map/all_to_all | solution.py:55
  91.6 4.9 %all-to-all-start.1 = ((bf16[1,16,24,1024]{3,2,0,1:T(8,128)(2,1)}), bf16[1,16,24,1024]{3,2,0,1:T(8,128)(2,1)S(1)}, u32[]{:S(2)}, u32[]{:S(2)}) async-start(bf16[1,16,24,1024]{3,2,0,1:T(8,128)(2,1)} %bitcast.7), calls=%async_computation.1 | async-start | bytes 1572864 | tf_op jit(solution)/shard_map/all_to_all | solution.py:62
  96.5 0.0 copy-start.8
  96.5 0.0 copy-done.5
  96.5 0.0 copy-start.7
  96.5 0.4 fusion.11
  96.9 9.9 %all-to-all-done.1 = bf16[1,16,24,1024]{3,2,0,1:T(8,128)(2,1)S(1)} async-done(((bf16[1,16,24,1024]{3,2,0,1:T(8,128)(2,1)}), bf16[1,16,24,1024]{3,2,0,1:T(8,128)(2,1)S(1)}, u32[]{:S(2)}, u32[]{:S(2)}) %all-to-all-start.1) | async-done | bytes 786464 | tf_op jit(solution)/shard_map/all_to_all | solution.py:62
  106.8 0.0 copy-done.1
  106.8 0.4 fusion.17
  107.2 0.7 reshape.184
  107.9 4.7 %all-to-all-start.4 = ((f32[1,16,24]{2,0,1:T(1,128)}), f32[1,16,24]{2,0,1:T(1,128)S(1)}, u32[]{:S(2)}, u32[]{:S(2)}) async-start(f32[1,16,24]{2,0,1:T(1,128)} %reshape.184), calls=%async_computation.6 | async-start | bytes 16384 | tf_op jit(solution)/shard_map/all_to_all | solution.py:100
  112.6 0.0 copy-done.8
  112.7 6.2 %all-to-all-done.4 = f32[1,16,24]{2,0,1:T(1,128)S(1)} async-done(((f32[1,16,24]{2,0,1:T(1,128)}), f32[1,16,24]{2,0,1:T(1,128)S(1)}, u32[]{:S(2)}, u32[]{:S(2)}) %all-to-all-start.4) | async-done | bytes 1568 | tf_op jit(solution)/shard_map/all_to_all | solution.py:100
  118.9 0.2 select_reduce_fusion
  119.0 0.0 copy-done.7
  119.0 0.1 select_reduce_fusion.2
  119.2 0.2 select_reduce_fusion.1
  119.4 10.6 %all_to_all.25 = bf16[1,16,24]{2,0,1:T(2,128)(2,1)S(1)} all-to-all(bf16[1,16,24]{2,0,1:T(2,128)(2,1)S(1)} %copy.45), channel_id=1, replica_groups=mesh['expert'=16,'hidden'=16] {'expert'}, dimensions={1} | all-to-all | bytes 1536 | tf_op jit(solution)/shard_map/all_to_all | solution.py:69
  130.0 0.1 reshape.185
  130.1 0.1 copy.48
  130.3 1.5 convolution_bitcast_fusion
  131.8 0.0 copy-start.2
  131.8 0.0 copy-start.4
  131.8 5.7 %all-to-all-start.3 = ((f32[1,16,24,1024]{3,2,0,1:T(8,128)}), f32[1,16,24,1024]{3,2,0,1:T(8,128)}, u32[]{:S(2)}, u32[]{:S(2)}) async-start(f32[1,16,24,1024]{3,2,0,1:T(8,128)} %convolution_bitcast_fusion), calls=%async_computation.3 | async-start | bytes 3145728 | tf_op jit(solution)/shard_map/all_to_all | solution.py:99
  137.5 0.0 reduce-scatter.5.cloned.1.call-start
  137.5 0.0 copy-done.2
  137.6 0.0 copy-done.4
  137.6 1.3 fusion.24
  138.9 0.0 reduce-scatter.5.cloned.1.call-update
  138.9 0.0 copy-start.6
  138.9 0.0 reduce-scatter.3.cloned.1.call-start
  139.0 13.1 %all-to-all-done.3 = f32[1,16,24,1024]{3,2,0,1:T(8,128)} async-done(((f32[1,16,24,1024]{3,2,0,1:T(8,128)}), f32[1,16,24,1024]{3,2,0,1:T(8,128)}, u32[]{:S(2)}, u32[]{:S(2)}) %all-to-all-start.3) | async-done | bytes 1572896 | tf_op jit(solution)/shard_map/all_to_all | solution.py:99
  152.1 3.5 %fusion.2 = f32[256,1024]{1,0:T(8,128)} fusion(f32[1,16,24,1024]{3,2,0,1:T(8,128)} %all-to-all-done.3, s32[16,256]{1,0:T(8,128)S(1)} %bitcast_subtract_fusion, pred[16,256]{1,0:T(8,128)(4,1)S(1)} %bitcast_compare_fusion.1), kind=kOutput, calls=%fused_computation.5 | convolution fusion | flops 1208156160 | bytes 2641920 | tf_op jit(solution)/shard_map/dot_general | solution.py:102
  155.7 66.5 %all-reduce.4 = (bf16[256,1024]{1,0:T(8,128)(2,1)S(1)}, f32[256,22]{0,1:T(8,128)}) all-reduce(f32[256,1024]{1,0:T(8,128)} %fusion.2, f32[256,22]{0,1:T(8,128)S(1)} %get-tuple-element.6), channel_id=1, replica_groups=mesh['expert'=16,'hidden'=16] {'hidden'}, use_global_device_ids=true, to_apply=%region_6.7 | all-reduce | flops 267776 | bytes 1617920 | tf_op jit(solution)/shard_map/psum | solution.py:111
  222.1 0.0 copy-done.6
  222.1 1.3 fusion.25
  223.5 0.0 reduce-scatter.3.cloned.1.call-update
  223.5 0.0 copy-start.3
  223.5 1.2 convolution_bitcast_fusion.2
  224.7 1.2 convolution_bitcast_fusion.1
  225.9 0.0 copy-done.3
  225.9 1.0 convolution_convert_fusion.2
  226.9 0.0 reduce-scatter.5.cloned.1.call-done
  226.9 79.2 %reduce-scatter.3.cloned.1.call-done = f32[64,256]{1,0:T(8,128)} async-done(((f32[1024,256]{1,0:T(8,128)}), f32[64,256]{1,0:T(8,128)}) %reduce-scatter.3.cloned.1.call-update) | async-done | bytes 65552 | tf_op jit(solution)/shard_map/reduce_scatter | solution.py:121
  (10 shorter events, 0.1 us)
Async XLA Ops:
  7.2 74.3 %copy-start = (bf16[256,1024]{1,0:T(8,128)(2,1)S(1)}, bf16[256,1024]{1,0:T(8,128)(2,1)}, u32[]{:S(2)}) copy-start(bf16[256,1024]{1,0:T(8,128)(2,1)} %param.12) | copy-start | bytes 1572868
  73.9 17.7 %all-to-all-start.2 = ((bf16[1,16,24,1024]{3,2,0,1:T(8,128)(2,1)}), bf16[1,16,24,1024]{3,2,0,1:T(8,128)(2,1)S(1)}, u32[]{:S(2)}, u32[]{:S(2)}) async-start(bf16[1,16,24,1024]{3,2,0,1:T(8,128)(2,1)} %bitcast.11), calls=%async_computation.2 | async-start | bytes 1572864 | tf_op jit(solution)/shard_map/all_to_all | solution.py:55
  81.4 15.1 %copy-start.5 = (bf16[1,168,1024]{2,1,0:T(8,128)(2,1)S(1)}, bf16[1,168,1024]{2,1,0:T(8,128)(2,1)}, u32[]{:S(2)}) copy-start(bf16[1,168,1024]{2,1,0:T(8,128)(2,1)} %param.19) | copy-start | bytes 1032196
  82.7 24.0 %copy-start.1 = (bf16[1,1024,168]{1,2,0:T(8,128)(2,1)S(1)}, bf16[1,1024,168]{1,2,0:T(8,128)(2,1)}, u32[]{:S(2)}) copy-start(bf16[1,1024,168]{1,2,0:T(8,128)(2,1)} %param.18) | copy-start | bytes 1032196
  91.6 15.2 %all-to-all-start.1 = ((bf16[1,16,24,1024]{3,2,0,1:T(8,128)(2,1)}), bf16[1,16,24,1024]{3,2,0,1:T(8,128)(2,1)S(1)}, u32[]{:S(2)}, u32[]{:S(2)}) async-start(bf16[1,16,24,1024]{3,2,0,1:T(8,128)(2,1)} %bitcast.7), calls=%async_computation.1 | async-start | bytes 1572864 | tf_op jit(solution)/shard_map/all_to_all | solution.py:62
  96.5 16.2 %copy-start.8 = (bf16[256,22]{0,1:T(8,128)(2,1)S(1)}, bf16[256,22]{0,1:T(8,128)(2,1)}, u32[]{:S(2)}) copy-start(bf16[256,22]{0,1:T(8,128)(2,1)} %param.15) | copy-start | bytes 33796
  96.5 22.5 %copy-start.7 = (s32[256,22]{0,1:T(8,128)S(1)}, s32[256,22]{0,1:T(8,128)}, u32[]{:S(2)}) copy-start(s32[256,22]{0,1:T(8,128)} %param.14) | copy-start | bytes 67588
  107.9 10.9 %all-to-all-start.4 = ((f32[1,16,24]{2,0,1:T(1,128)}), f32[1,16,24]{2,0,1:T(1,128)S(1)}, u32[]{:S(2)}, u32[]{:S(2)}) async-start(f32[1,16,24]{2,0,1:T(1,128)} %reshape.184), calls=%async_computation.6 | async-start | bytes 16384 | tf_op jit(solution)/shard_map/all_to_all | solution.py:100
  131.8 5.8 %copy-start.2 = (bf16[256,1024]{1,0:T(8,128)(2,1)S(1)}, bf16[256,1024]{1,0:T(8,128)(2,1)}, u32[]{:S(2)}) copy-start(bf16[256,1024]{1,0:T(8,128)(2,1)} %param.13) | copy-start | bytes 1572868
  131.8 5.8 %copy-start.4 = (bf16[256,256]{1,0:T(8,128)(2,1)S(1)}, bf16[256,256]{1,0:T(8,128)(2,1)}, u32[]{:S(2)}) copy-start(bf16[256,256]{1,0:T(8,128)(2,1)} %param.11) | copy-start | bytes 393220
  131.8 20.3 %all-to-all-start.3 = ((f32[1,16,24,1024]{3,2,0,1:T(8,128)}), f32[1,16,24,1024]{3,2,0,1:T(8,128)}, u32[]{:S(2)}, u32[]{:S(2)}) async-start(f32[1,16,24,1024]{3,2,0,1:T(8,128)} %convolution_bitcast_fusion), calls=%async_computation.3 | async-start | bytes 3145728 | tf_op jit(solution)/shard_map/all_to_all | solution.py:99
  137.5 89.4 %reduce-scatter.5.cloned.1.call-start = ((), (), s32[]{:S(2)}) async-start(), calls=%async_computation.8 | async-start | bytes 1114112 | tf_op jit(solution)/shard_map/reduce_scatter | solution.py:122
  138.9 83.2 %copy-start.6 = (bf16[256,256]{1,0:T(8,128)(2,1)S(1)}, bf16[256,256]{1,0:T(8,128)(2,1)}, u32[]{:S(2)}) copy-start(bf16[256,256]{1,0:T(8,128)(2,1)} %param.10) | copy-start | bytes 393220
  138.9 167.1 %reduce-scatter.3.cloned.1.call-start = ((), (), s32[]{:S(2)}) async-start(), calls=%async_computation.7 | async-start | bytes 1114112 | tf_op jit(solution)/shard_map/reduce_scatter | solution.py:121
  223.5 2.4 copy-start.3
Sparse Core Ops, SparseCore 0:
  142.4 81.0 reduce-scatter.4
  227.6 78.4 reduce-scatter.2
where the time goes:
time: 313 us
  blocking collectives  139 us (44%)
  waiting for transfers between devices  117 us (37%)
  starting transfers between devices  22.9 us (7%)
  matrix products  15.9 us (5%)
  between operations  14.3 us (5%)
    reduce_scatter x1, waiting for transfers between devices, on_device(): lax.psum_scatter(down_term, 'expert', scatter_dimension=0, tiled=True)  79.2 us
    psum x1, blocking collectives, on_device(): latent_grad, gate_grad = lax.psum((token_sums, gate_local), 'hidden')  66.5 us
    psum x1, blocking collectives, on_device(): cot_full = lax.psum(partial_cot, 'hidden')  62 us
    all_to_all x1, waiting for transfers between devices, on_device(): lax.all_to_all(latent_back, 'expert', split_axis=1, concat_axis=1, tiled=...  13.1 us
    all_to_all x1, blocking collectives, on_device(): lax.all_to_all(gate_send, 'expert', split_axis=1, concat_axis=1, tiled=True)  10.6 us
    all_to_all x1, waiting for transfers between devices, on_device(): lax.all_to_all(latent_rows.reshape(local_count, groups, capacity, latent_...  9.86 us
    all_to_all x1, waiting for transfers between devices, on_device(): lax.all_to_all(cot_rows.reshape(local_count, groups, capacity, latent_wid...  8.87 us
    all_to_all x1, starting transfers between devices, on_device(): lax.all_to_all(cot_rows.reshape(local_count, groups, capacity, latent_wid...  7.48 us
  transfers between devices with their start and end apart: 6, of which 5 were waited for; matrix products, arithmetic and copies ran while one was open for 4% of the time, Pallas kernels for 0%

commit v1 on v0

--- a/solution.py
+++ b/solution.py
@@ -44,7 +44,11 @@
     )
     gate_send = gate_slot.astype(jnp.bfloat16)
     dispatch_bf = hit_slot.astype(jnp.bfloat16).reshape(slot_total, tokens_here)
-    cot_full = lax.psum(partial_cot, "hidden")
+    cot_full = partial_cot
+    for hop in (1, 2, 4, 8):
+        cot_full = cot_full + lax.ppermute(
+            cot_full, "hidden", [(dev, dev ^ hop) for dev in range(16)]
+        )
     cot_rows = jnp.dot(
         dispatch_bf, cot_full.astype(jnp.bfloat16), preferred_element_type=jnp.float32
     ).astype(jnp.bfloat16)

time: 313 us -> 379 us (1.21)
  waiting for transfers between devices: 117 us -> 239 us
  blocking collectives: 139 us -> 71.8 us
  starting transfers between devices: 22.9 us -> 34.6 us
    ppermute x0 -> x4, waiting for transfers between devices: none -> 116 us  [on_device(): lax.ppermute(cot_full, 'hidden', [(dev, dev ^ hop) for dev in range(16)])]
    psum x1 -> x0, blocking collectives: 62 us -> none  [on_device(): cot_full = lax.psum(partial_cot, 'hidden')]
    ppermute x0 -> x4, starting transfers between devices: none -> 11.8 us  [on_device(): lax.ppermute(cot_full, 'hidden', [(dev, dev ^ hop) for dev in range(16)])]
    psum x1, blocking collectives: 66.5 us -> 61.3 us  [on_device(): latent_grad, gate_grad = lax.psum((token_sums, gate_local), 'hidden')]
  transfers between devices with their start and end apart: 6 -> 10, of which waited for: 5 -> 9; matrix products, arithmetic and copies ran while one was open for 4% -> 3% of each run, Pallas kernels for 0% -> 0%
where the time goes in v1:
time: 379 us
  waiting for transfers between devices  239 us (63%)
  blocking collectives  71.8 us (19%)
  starting transfers between devices  34.6 us (9%)
  matrix products  16 us (4%)
  between operations  14.3 us (4%)
    ppermute x4, waiting for transfers between devices, on_device(): lax.ppermute(cot_full, 'hidden', [(dev, dev ^ hop) for dev in range(16)])  116 us
    reduce_scatter x1, waiting for transfers between devices, on_device(): lax.psum_scatter(down_term, 'expert', scatter_dimension=0, tiled=True)  79.2 us
    psum x1, blocking collectives, on_device(): latent_grad, gate_grad = lax.psum((token_sums, gate_local), 'hidden')  61.3 us
    all_to_all x1, waiting for transfers between devices, on_device(): lax.all_to_all(latent_back, 'expert', split_axis=1, concat_axis=1, tiled=...  15.6 us
    ppermute x4, starting transfers between devices, on_device(): lax.ppermute(cot_full, 'hidden', [(dev, dev ^ hop) for dev in range(16)])  11.8 us
    all_to_all x1, waiting for transfers between devices, on_device(): lax.all_to_all(latent_rows.reshape(local_count, groups, capacity, latent_...  11 us
    all_to_all x1, waiting for transfers between devices, on_device(): lax.all_to_all(cot_rows.reshape(local_count, groups, capacity, latent_wid...  10.8 us
    all_to_all x1, blocking collectives, on_device(): lax.all_to_all(gate_send, 'expert', split_axis=1, concat_axis=1, tiled=True)  10.6 us
  transfers between devices with their start and end apart: 10, of which 9 were waited for; matrix products, arithmetic and copies ran while one was open for 3% of the time, Pallas kernels for 0%

profile of v1, /device:TPU:2, one launch (start us, length us, event | category | flops | bytes accessed | tf_op | source)
XLA Modules:
  0.0 378.6 jit_solution(8667762502702058519)
XLA Ops:
  7.2 0.0 copy-start
  7.2 1.5 fusion.22
  8.7 0.1 collective-permute-start
  8.8 2.6 collective-permute-done
  11.4 0.1 add.20
  11.6 2.0 collective-permute-start.1
  13.6 23.5 %collective-permute-done.1 = f32[256,1024]{1,0:T(8,128)S(1)} collective-permute-done((f32[256,1024]{1,0:T(8,128)S(1)}, f32[256,1024]{1,0:T(8,128)S(1)}, u32[]{:S(2)}, u32[]{:S(2)}) %collective-permute-start.1) | collective-permute-done | bytes 1048608 | tf_op jit(solution)/shard_map/ppermute | solution.py:49
  37.0 0.2 add.21
  37.2 0.0 copy-start.7
  37.2 3.4 collective-permute-start.2
  40.6 45.2 %collective-permute-done.2 = f32[256,1024]{1,0:T(8,128)S(1)} collective-permute-done((f32[256,1024]{1,0:T(8,128)S(1)}, f32[256,1024]{1,0:T(8,128)S(1)}, u32[]{:S(2)}, u32[]{:S(2)}) %collective-permute-start.2) | collective-permute-done | bytes 1048608 | tf_op jit(solution)/shard_map/ppermute | solution.py:49
  85.8 0.1 add.22
  86.0 6.3 %collective-permute-start.3 = (f32[256,1024]{1,0:T(8,128)S(1)}, f32[256,1024]{1,0:T(8,128)S(1)}, u32[]{:S(2)}, u32[]{:S(2)}) collective-permute-start(f32[256,1024]{1,0:T(8,128)S(1)} %add.22), channel_id=1, source_target_pairs={{0,8},{1,9},{2,10},{3,11},{4,12},{5,13},{6,14},{7,15},{8,0},{9,1},... | collective-permute-start | bytes 3145736 | tf_op jit(solution)/shard_map/ppermute | solution.py:49
  92.3 0.1 eq.79
  92.3 0.0 copy-done.7
  92.4 0.6 reduce-window.6
  93.0 0.2 slice_reduce_fusion
  93.2 0.1 bitcast_subtract_fusion
  93.3 0.1 fusion.8
  93.5 44.6 %collective-permute-done.3 = f32[256,1024]{1,0:T(8,128)S(1)} collective-permute-done((f32[256,1024]{1,0:T(8,128)S(1)}, f32[256,1024]{1,0:T(8,128)S(1)}, u32[]{:S(2)}, u32[]{:S(2)}) %collective-permute-start.3) | collective-permute-done | bytes 1048608 | tf_op jit(solution)/shard_map/ppermute | solution.py:49
  138.1 1.3 convolution_convert_fusion
  139.3 7.5 %all-to-all-start.2 = ((bf16[1,16,24,1024]{3,2,0,1:T(8,128)(2,1)}), bf16[1,16,24,1024]{3,2,0,1:T(8,128)(2,1)S(1)}, u32[]{:S(2)}, u32[]{:S(2)}) async-start(bf16[1,16,24,1024]{3,2,0,1:T(8,128)(2,1)} %bitcast.11), calls=%async_computation.2 | async-start | bytes 1572864 | tf_op jit(solution)/shard_map/all_to_all | solution.py:59
  146.8 0.0 copy-done
  146.8 0.0 copy-start.5
  146.8 1.3 convolution_convert_fusion.1
  148.1 0.0 copy-start.1
  148.1 10.8 %all-to-all-done.2 = bf16[1,16,24,1024]{3,2,0,1:T(8,128)(2,1)S(1)} async-done(((bf16[1,16,24,1024]{3,2,0,1:T(8,128)(2,1)}), bf16[1,16,24,1024]{3,2,0,1:T(8,128)(2,1)S(1)}, u32[]{:S(2)}, u32[]{:S(2)}) %all-to-all-start.2) | async-done | bytes 786464 | tf_op jit(solution)/shard_map/all_to_all | solution.py:59
  158.9 4.9 %all-to-all-start.1 = ((bf16[1,16,24,1024]{3,2,0,1:T(8,128)(2,1)}), bf16[1,16,24,1024]{3,2,0,1:T(8,128)(2,1)S(1)}, u32[]{:S(2)}, u32[]{:S(2)}) async-start(bf16[1,16,24,1024]{3,2,0,1:T(8,128)(2,1)} %bitcast.7), calls=%async_computation.1 | async-start | bytes 1572864 | tf_op jit(solution)/shard_map/all_to_all | solution.py:66
  163.8 0.0 copy-done.5
  163.8 0.4 fusion.10
  164.2 11.0 %all-to-all-done.1 = bf16[1,16,24,1024]{3,2,0,1:T(8,128)(2,1)S(1)} async-done(((bf16[1,16,24,1024]{3,2,0,1:T(8,128)(2,1)}), bf16[1,16,24,1024]{3,2,0,1:T(8,128)(2,1)S(1)}, u32[]{:S(2)}, u32[]{:S(2)}) %all-to-all-start.1) | async-done | bytes 786464 | tf_op jit(solution)/shard_map/all_to_all | solution.py:66
  175.2 0.0 copy-done.1
  175.2 0.5 fusion.16
  175.7 0.7 reshape.184
  176.4 4.7 %all-to-all-start.4 = ((f32[1,16,24]{2,0,1:T(1,128)}), f32[1,16,24]{2,0,1:T(1,128)S(1)}, u32[]{:S(2)}, u32[]{:S(2)}) async-start(f32[1,16,24]{2,0,1:T(1,128)} %reshape.184), calls=%async_computation.6 | async-start | bytes 16384 | tf_op jit(solution)/shard_map/all_to_all | solution.py:104
  181.1 0.0 copy-done.8
  181.1 6.2 %all-to-all-done.4 = f32[1,16,24]{2,0,1:T(1,128)S(1)} async-done(((f32[1,16,24]{2,0,1:T(1,128)}), f32[1,16,24]{2,0,1:T(1,128)S(1)}, u32[]{:S(2)}, u32[]{:S(2)}) %all-to-all-start.4) | async-done | bytes 1568 | tf_op jit(solution)/shard_map/all_to_all | solution.py:104
  187.3 0.2 select_reduce_fusion
  187.5 0.1 select_reduce_fusion.2
  187.6 0.2 select_reduce_fusion.1
  187.8 10.6 %all_to_all.25 = bf16[1,16,24]{2,0,1:T(2,128)(2,1)S(1)} all-to-all(bf16[1,16,24]{2,0,1:T(2,128)(2,1)S(1)} %copy.45), channel_id=1, replica_groups=mesh['expert'=16,'hidden'=16] {'expert'}, dimensions={1} | all-to-all | bytes 1536 | tf_op jit(solution)/shard_map/all_to_all | solution.py:73
  198.4 0.1 reshape.185
  198.5 0.1 copy.48
  198.7 1.5 convolution_bitcast_fusion
  200.2 5.7 %all-to-all-start.3 = ((f32[1,16,24,1024]{3,2,0,1:T(8,128)}), f32[1,16,24,1024]{3,2,0,1:T(8,128)}, u32[]{:S(2)}, u32[]{:S(2)}) async-start(f32[1,16,24,1024]{3,2,0,1:T(8,128)} %convolution_bitcast_fusion), calls=%async_computation.3 | async-start | bytes 3145728 | tf_op jit(solution)/shard_map/all_to_all | solution.py:103
  205.9 0.0 reduce-scatter.5.cloned.1.call-start
  206.0 0.0 copy-done.2
  206.0 0.0 copy-done.4
  206.0 1.3 fusion.23
  207.3 0.0 reduce-scatter.5.cloned.1.call-update
  207.3 0.0 copy-start.6
  207.3 0.0 reduce-scatter.3.cloned.1.call-start
  207.4 15.6 %all-to-all-done.3 = f32[1,16,24,1024]{3,2,0,1:T(8,128)} async-done(((f32[1,16,24,1024]{3,2,0,1:T(8,128)}), f32[1,16,24,1024]{3,2,0,1:T(8,128)}, u32[]{:S(2)}, u32[]{:S(2)}) %all-to-all-start.3) | async-done | bytes 1572896 | tf_op jit(solution)/shard_map/all_to_all | solution.py:103
  223.0 3.5 fusion.2
  226.5 61.3 %all-reduce.2 = (bf16[256,1024]{1,0:T(8,128)(2,1)S(1)}, f32[256,22]{0,1:T(8,128)}) all-reduce(f32[256,1024]{1,0:T(8,128)} %fusion.2, f32[256,22]{0,1:T(8,128)S(1)} %get-tuple-element.6), channel_id=1, replica_groups=mesh['expert'=16,'hidden'=16] {'hidden'}, use_global_device_ids=true, to_apply=%region_5.6 | all-reduce | flops 267776 | bytes 1617920 | tf_op jit(solution)/shard_map/psum | solution.py:115
  287.7 0.0 copy-done.6
  287.8 1.3 fusion.24
  289.1 0.0 reduce-scatter.3.cloned.1.call-update
  289.1 0.0 copy-start.3
  289.1 1.2 convolution_bitcast_fusion.2
  290.3 1.2 convolution_bitcast_fusion.1
  291.5 0.0 copy-done.3
  291.5 1.0 convolution_convert_fusion.2
  292.5 79.2 %reduce-scatter.3.cloned.1.call-done = f32[64,256]{1,0:T(8,128)} async-done(((f32[1024,256]{1,0:T(8,128)}), f32[64,256]{1,0:T(8,128)}) %reduce-scatter.3.cloned.1.call-update) | async-done | bytes 65552 | tf_op jit(solution)/shard_map/reduce_scatter | solution.py:125
  (15 shorter events, 0.2 us)
Async XLA Ops:
  7.2 139.7 %copy-start = (bf16[256,1024]{1,0:T(8,128)(2,1)S(1)}, bf16[256,1024]{1,0:T(8,128)(2,1)}, u32[]{:S(2)}) copy-start(bf16[256,1024]{1,0:T(8,128)(2,1)} %param.12) | copy-start | bytes 1572868
  8.7 2.7 collective-permute-start
  11.6 25.5 %collective-permute-start.1 = (f32[256,1024]{1,0:T(8,128)S(1)}, f32[256,1024]{1,0:T(8,128)S(1)}, u32[]{:S(2)}, u32[]{:S(2)}) collective-permute-start(f32[256,1024]{1,0:T(8,128)S(1)} %add.20), channel_id=1, source_target_pairs={{0,2},{1,3},{2,0},{3,1},{4,6},{5,7},{6,4},{7,5},{8,10},{9,11},{10,... | collective-permute-start | bytes 3145736 | tf_op jit(solution)/shard_map/ppermute | solution.py:49
  37.2 55.2 %copy-start.7 = (s32[256,22]{0,1:T(8,128)S(1)}, s32[256,22]{0,1:T(8,128)}, u32[]{:S(2)}) copy-start(s32[256,22]{0,1:T(8,128)} %param.14) | copy-start | bytes 67588
  37.2 48.6 %collective-permute-start.2 = (f32[256,1024]{1,0:T(8,128)S(1)}, f32[256,1024]{1,0:T(8,128)S(1)}, u32[]{:S(2)}, u32[]{:S(2)}) collective-permute-start(f32[256,1024]{1,0:T(8,128)S(1)} %add.21), channel_id=1, source_target_pairs={{0,4},{1,5},{2,6},{3,7},{4,0},{5,1},{6,2},{7,3},{8,12},{9,13},{10,... | collective-permute-start | bytes 3145736 | tf_op jit(solution)/shard_map/ppermute | solution.py:49
  86.0 52.1 %collective-permute-start.3 = (f32[256,1024]{1,0:T(8,128)S(1)}, f32[256,1024]{1,0:T(8,128)S(1)}, u32[]{:S(2)}, u32[]{:S(2)}) collective-permute-start(f32[256,1024]{1,0:T(8,128)S(1)} %add.22), channel_id=1, source_target_pairs={{0,8},{1,9},{2,10},{3,11},{4,12},{5,13},{6,14},{7,15},{8,0},{9,1},... | collective-permute-start | bytes 3145736 | tf_op jit(solution)/shard_map/ppermute | solution.py:49
  139.3 19.6 %all-to-all-start.2 = ((bf16[1,16,24,1024]{3,2,0,1:T(8,128)(2,1)}), bf16[1,16,24,1024]{3,2,0,1:T(8,128)(2,1)S(1)}, u32[]{:S(2)}, u32[]{:S(2)}) async-start(bf16[1,16,24,1024]{3,2,0,1:T(8,128)(2,1)} %bitcast.11), calls=%async_computation.2 | async-start | bytes 1572864 | tf_op jit(solution)/shard_map/all_to_all | solution.py:59
  146.8 17.0 %copy-start.5 = (bf16[1,168,1024]{2,1,0:T(8,128)(2,1)S(1)}, bf16[1,168,1024]{2,1,0:T(8,128)(2,1)}, u32[]{:S(2)}) copy-start(bf16[1,168,1024]{2,1,0:T(8,128)(2,1)} %param.19) | copy-start | bytes 1032196
  148.1 27.1 %copy-start.1 = (bf16[1,1024,168]{1,2,0:T(8,128)(2,1)S(1)}, bf16[1,1024,168]{1,2,0:T(8,128)(2,1)}, u32[]{:S(2)}) copy-start(bf16[1,1024,168]{1,2,0:T(8,128)(2,1)} %param.18) | copy-start | bytes 1032196
  158.9 16.3 %all-to-all-start.1 = ((bf16[1,16,24,1024]{3,2,0,1:T(8,128)(2,1)}), bf16[1,16,24,1024]{3,2,0,1:T(8,128)(2,1)S(1)}, u32[]{:S(2)}, u32[]{:S(2)}) async-start(bf16[1,16,24,1024]{3,2,0,1:T(8,128)(2,1)} %bitcast.7), calls=%async_computation.1 | async-start | bytes 1572864 | tf_op jit(solution)/shard_map/all_to_all | solution.py:66
  163.8 17.3 %copy-start.8 = (bf16[256,22]{0,1:T(8,128)(2,1)S(1)}, bf16[256,22]{0,1:T(8,128)(2,1)}, u32[]{:S(2)}) copy-start(bf16[256,22]{0,1:T(8,128)(2,1)} %param.15) | copy-start | bytes 33796
  176.4 10.9 %all-to-all-start.4 = ((f32[1,16,24]{2,0,1:T(1,128)}), f32[1,16,24]{2,0,1:T(1,128)S(1)}, u32[]{:S(2)}, u32[]{:S(2)}) async-start(f32[1,16,24]{2,0,1:T(1,128)} %reshape.184), calls=%async_computation.6 | async-start | bytes 16384 | tf_op jit(solution)/shard_map/all_to_all | solution.py:104
  200.2 5.8 %copy-start.2 = (bf16[256,1024]{1,0:T(8,128)(2,1)S(1)}, bf16[256,1024]{1,0:T(8,128)(2,1)}, u32[]{:S(2)}) copy-start(bf16[256,1024]{1,0:T(8,128)(2,1)} %param.13) | copy-start | bytes 1572868
  200.2 5.8 %copy-start.4 = (bf16[256,256]{1,0:T(8,128)(2,1)S(1)}, bf16[256,256]{1,0:T(8,128)(2,1)}, u32[]{:S(2)}) copy-start(bf16[256,256]{1,0:T(8,128)(2,1)} %param.11) | copy-start | bytes 393220
  200.2 22.8 %all-to-all-start.3 = ((f32[1,16,24,1024]{3,2,0,1:T(8,128)}), f32[1,16,24,1024]{3,2,0,1:T(8,128)}, u32[]{:S(2)}, u32[]{:S(2)}) async-start(f32[1,16,24,1024]{3,2,0,1:T(8,128)} %convolution_bitcast_fusion), calls=%async_computation.3 | async-start | bytes 3145728 | tf_op jit(solution)/shard_map/all_to_all | solution.py:103
  205.9 86.6 %reduce-scatter.5.cloned.1.call-start = ((), (), s32[]{:S(2)}) async-start(), calls=%async_computation.8 | async-start | bytes 1114112 | tf_op jit(solution)/shard_map/reduce_scatter | solution.py:126
  207.3 80.4 %copy-start.6 = (bf16[256,256]{1,0:T(8,128)(2,1)S(1)}, bf16[256,256]{1,0:T(8,128)(2,1)}, u32[]{:S(2)}) copy-start(bf16[256,256]{1,0:T(8,128)(2,1)} %param.10) | copy-start | bytes 393220
  207.3 164.4 %reduce-scatter.3.cloned.1.call-start = ((), (), s32[]{:S(2)}) async-start(), calls=%async_computation.7 | async-start | bytes 1114112 | tf_op jit(solution)/shard_map/reduce_scatter | solution.py:125
  289.1 2.4 copy-start.3
Sparse Core Ops, SparseCore 0:
  210.8 78.3 reduce-scatter.4
  293.3 78.4 reduce-scatter.2
